TPU v7x, 32 devices: a whole 2x2x4 slice. The times are simulated.
32 devices in a mesh: grp: 4 (over y, x), lm: 8 (over z, core).
Axes of the slice: x: 2, y: 2, z: 4, core: 2. Of those that a mesh axis runs over, the one named last changes fastest.
Arguments:
- embeddings: bfloat16 [8192, 512], P(('grp', 'lm')), may hold values from -14 to 14
- landmarks: bfloat16 [16384, 512], P('lm'), may hold values from -14 to 14
- start_vectors: float32 [8192, 128], P(('grp', 'lm')), may hold values from -10 to 10
- row_weight: float32 [8192], P(('grp', 'lm')), may hold values from 0.1 to 9
- spread: float32 [1], replicated, may hold values from 11.313708 to 33.941124
Outputs:
- subspace: float32 [8192, 128], P(('grp', 'lm'))
All inputs are finite; a program needn't handle non-finite values.
Results may differ from a plain program's by a relative error of at most 0.019.
Values may be sent and summed in bfloat16 or wider, within the bound.
A program may use at most 128 MiB of HBM per device.

v0:
```python
import jax
import jax.numpy as jnp
from jax import lax
from jax.sharding import PartitionSpec as P

ITERS = 2


def unit_rows(values):
    values = values.astype(jnp.float32)
    scale = lax.rsqrt(jnp.sum(values * values, axis=1, keepdims=True) + 1e-06)
    return (values * scale).astype(jnp.bfloat16)


def kernel_values(rows_unit, marks_unit, gamma):
    cosine = jnp.einsum("rd,ld->rl", rows_unit, marks_unit, preferred_element_type=jnp.float32)
    return jnp.exp(gamma * cosine)


def local(embeddings, landmarks, start_vectors, row_weight, spread):
    own_rows = embeddings.shape[0]
    marks = landmarks.shape[0]
    groups = lax.axis_size("grp")
    members = lax.axis_size("lm")
    total_rows = own_rows * groups * members
    group_rows = own_rows * members
    gamma = spread[0]
    rows_unit = unit_rows(embeddings)
    marks_unit = unit_rows(landmarks)
    sums = jnp.zeros((marks,), jnp.float32)
    weights = jnp.zeros((group_rows,), jnp.float32)
    part_rows = lax.all_gather(rows_unit, "lm", axis=0, tiled=True)
    part_weight = lax.all_gather(row_weight.astype(jnp.bfloat16), "lm", axis=0, tiled=True).astype(
        jnp.float32
    )
    values = kernel_values(part_rows, marks_unit, gamma)
    build_tile = values.astype(jnp.bfloat16)
    weights = lax.dynamic_update_slice_in_dim(weights, part_weight, jnp.int32(0), 0)
    sums = sums + jnp.sum(part_weight[:, None] * values, axis=0)
    mean_sum, weight_sum = lax.psum((sums, jnp.sum(weights)), "grp")
    means = mean_sum / weight_sum
    vectors = start_vectors
    weighted_full = row_weight[:, None] * vectors
    totals = lax.psum(jnp.sum(weighted_full, axis=0), ("grp", "lm"))
    group_weighted = lax.all_gather(weighted_full.astype(jnp.bfloat16), "lm", axis=0, tiled=True)
    for step in range(ITERS):
        side = (
            lax.psum(
                jnp.einsum(
                    "rl,rv->lv", build_tile, group_weighted, preferred_element_type=jnp.float32
                ),
                "grp",
            )
            - means[:, None] * totals[None, :]
        )
        side_b = side.astype(jnp.bfloat16)
        shift = jnp.dot(means, side_b.astype(jnp.float32), precision=lax.Precision.HIGHEST)
        partial_rows = weights[:, None] * (
            jnp.dot(build_tile, side_b, preferred_element_type=jnp.float32) - shift[None, :]
        )
        image = lax.psum(partial_rows, "lm")
        square, column = lax.psum(
            (jnp.sum(image * image, axis=0), jnp.sum(weights[:, None] * image, axis=0)), "grp"
        )
        scale = jnp.sqrt(square / total_rows + 1e-06)
        group_vectors = image / scale[None, :]
        totals = column / scale
        group_weighted = (weights[:, None] * group_vectors).astype(jnp.bfloat16)
        vectors = lax.dynamic_slice_in_dim(
            group_vectors, lax.axis_index("lm") * own_rows, own_rows, 0
        )
    return vectors


def solution(mesh):
    in_specs = (
        P(("grp", "lm"), None),
        P("lm", None),
        P(("grp", "lm"), None),
        P(("grp", "lm")),
        P(),
    )
    out_specs = P(("grp", "lm"), None)
    return jax.shard_map(local, mesh=mesh, in_specs=in_specs, out_specs=out_specs, check_vma=False)
```

profile of v0, /device:TPU:0, one launch (start us, length us, event | category | flops | bytes accessed | tf_op | source)
XLA Modules:
  0.0 337.8 jit_solution(3544346859675565320)
XLA Ops:
  6.5 1.1 fusion.8
  7.6 1.8 fusion.9
  10.2 13.5 %all-gather = bf16[8,1,256]{2,1,0:T(2,128)(2,1)S(1)} all-gather(bf16[1,1,256]{2,1,0:T(2,128)(2,1)S(1)} %reshape.21), channel_id=1, replica_groups=mesh['grp'=4,'lm'=8] {'lm'}, dimensions={0}, use_global_device_ids=true | all-gather | bytes 4608 | tf_op jit(solution)/shard_map/all_gather | solution.py:33
  24.3 2.1 fusion.1
  26.4 1.0 multiply_reduce_fusion.4
  27.4 17.3 %all_gather.11 = bf16[2048,128]{1,0:T(8,128)(2,1)S(1)} all-gather(bf16[256,128]{1,0:T(8,128)(2,1)S(1)} %get-tuple-element.14), channel_id=1, replica_groups=mesh['grp'=4,'lm'=8] {'lm'}, dimensions={0}, use_global_device_ids=true | all-gather | bytes 589824 | tf_op jit(solution)/shard_map/all_gather | solution.py:45
  45.7 7.8 %multiply_reduce_fusion = (f32[2048]{0:T(1024)S(1)}, bf16[2048,2048]{1,0:T(8,128)(2,1)S(1)}) fusion(f32[2048]{0:T(1024)S(1)} %bitcast.19, f32[]{:T(128)} %bitcast.16, bf16[2048,512]{1,0:T(8,128)(2,1)} %all-gather.3.cloned.1.call-done, bf16[2048,512]{1,0:T(8,128)(2,1)} %param.6, f32[2048]{0:T(1024)S(1)} %add_rsqrt_fusion), kind=kOutput, calls=%fused_computation | convolution fusion | flops 4314888192 | bytes 12607492 | tf_op jit(solution)/shard_map/rd,ld->rl/dot_general | solution.py:16
  53.5 3.2 copy-done
  56.7 3.4 %fusion.14 = f32[2048,128]{1,0:T(8,128)} fusion(bf16[2048,2048]{1,0:T(8,128)(2,1)S(1)} %get-tuple-element.12, bf16[2048,128]{1,0:T(8,128)(2,1)S(1)} %all_gather.11), kind=kOutput, calls=%fused_computation.38 | convolution fusion | flops 1073741824 | bytes 9961472 | tf_op jit(solution)/shard_map/rl,rv->lv/dot_general | solution.py:49
  60.2 40.3 %psum.73 = f32[128]{0:T(128)S(1)} all-reduce(f32[128]{0:T(128)S(1)} %get-tuple-element.13), channel_id=1, replica_groups=mesh['grp'=4,'lm'=8] {'grp','lm'}, use_global_device_ids=true, to_apply=%region_8.0 | all-reduce | flops 128 | bytes 1024 | tf_op jit(solution)/shard_map/psum | solution.py:44
  101.1 11.7 %all-reduce.1 = (f32[2048]{0:T(1024)S(1)}, f32[]{:T(128)}) all-reduce(f32[2048]{0:T(1024)S(1)} %get-tuple-element.11, f32[]{:T(128)} %convert_reduce_fusion), channel_id=1, replica_groups=mesh['grp'=4,'lm'=8] {'grp'}, use_global_device_ids=true, to_apply=%region_4.0 | all-reduce | flops 2049 | bytes 16392 | tf_op jit(solution)/shard_map/psum | solution.py:40
  113.5 1.8 convolution_bitcast_fusion.1
  115.3 7.1 %fusion.4 = f32[2048,128]{1,0:T(8,128)} fusion(bf16[2048,2048]{1,0:T(8,128)(2,1)} %copy-done, f32[128]{0:T(128)S(1)} %convolution_bitcast_fusion.1, f32[2048]{0:T(1024)S(1)} %bitcast.20, f32[2048,128]{1,0:T(8,128)} %all-reduce.7.cloned.1.call-done, f32[128]{0:T(128)S(1)} %psum.73, f32[2048]{0:T(1024)S(1)} %broadcast_divide_fusion), kind=kOutput, calls=%fused_computation.10 | convolution fusion | flops 1075052544 | bytes 10503168 | tf_op jit(solution)/shard_map/dot_general | solution.py:59
  122.5 58.7 %all-reduce.9.cloned.1.call-done = f32[2048,128]{1,0:T(8,128)} async-done(((f32[2048,128]{1,0:T(8,128)}), f32[2048,128]{1,0:T(8,128)}) %all-reduce.9.cloned.1.call-update) | async-done | bytes 1048592 | tf_op jit(solution)/shard_map/psum | solution.py:61
  181.1 1.6 multiply_reduce_fusion.2
  182.7 10.0 %all-reduce = (f32[128]{0:T(128)S(1)}, f32[128]{0:T(128)S(1)}) all-reduce(f32[128]{0:T(128)S(1)} %get-tuple-element.6, f32[128]{0:T(128)S(1)} %get-tuple-element.5), channel_id=1, replica_groups=mesh['grp'=4,'lm'=8] {'grp'}, use_global_device_ids=true, to_apply=%region_11.0 | all-reduce | flops 256 | bytes 2048 | tf_op jit(solution)/shard_map/psum | solution.py:62
  192.7 7.3 %fusion.10 = f32[2048,128]{1,0:T(8,128)} fusion(bf16[2048,2048]{1,0:T(8,128)(2,1)} %copy-done, f32[2048,128]{1,0:T(8,128)} %all-reduce.9.cloned.1.call-done, f32[128]{0:T(128)S(1)} %get-tuple-element.16, f32[2048]{0:T(1024)S(1)} %bitcast.22), kind=kOutput, calls=%fused_computation.25 | convolution fusion | flops 1074528256 | bytes 10494464 | tf_op jit(solution)/shard_map/rl,rv->lv/dot_general | solution.py:49
  200.1 49.9 %all-reduce.11.cloned.1.call-done = f32[2048,128]{1,0:T(8,128)} async-done(((f32[2048,128]{1,0:T(8,128)}), f32[2048,128]{1,0:T(8,128)}) %all-reduce.11.cloned.1.call-update) | async-done | bytes 1048592 | tf_op jit(solution)/shard_map/psum | solution.py:48
  250.0 1.8 convolution_bitcast_fusion
  251.8 7.1 %fusion.3 = f32[2048,128]{1,0:T(8,128)} fusion(bf16[2048,2048]{1,0:T(8,128)(2,1)} %copy-done, f32[128]{0:T(128)S(1)} %convolution_bitcast_fusion, f32[2048]{0:T(1024)S(1)} %bitcast.23, f32[2048,128]{1,0:T(8,128)} %all-reduce.11.cloned.1.call-done, f32[128]{0:T(128)S(1)} %get-tuple-element.15, f32[2048]{0:T(1024)S(1)} %broadcast_divide_fusion), kind=kOutput, calls=%fused_computation.8 | convolution fusion | flops 1075052544 | bytes 10503168 | tf_op jit(solution)/shard_map/dot_general | solution.py:59
  258.9 59.5 %all-reduce.13.cloned.1.call-done = f32[2048,128]{1,0:T(8,128)} async-done(((f32[2048,128]{1,0:T(8,128)}), f32[2048,128]{1,0:T(8,128)}) %all-reduce.13.cloned.1.call-update) | async-done | bytes 1048592 | tf_op jit(solution)/shard_map/psum | solution.py:61
  318.4 1.5 multiply_reduce_fusion.1
  319.9 9.8 %psum.79 = f32[128]{0:T(128)S(1)} all-reduce(f32[128]{0:T(128)S(1)} %multiply_reduce_fusion.1), channel_id=1, replica_groups=mesh['grp'=4,'lm'=8] {'grp'}, use_global_device_ids=true, to_apply=%region_17.0 | all-reduce | flops 128 | bytes 1024 | tf_op jit(solution)/shard_map/psum | solution.py:62
  329.7 1.6 dynamic-slice_divide_fusion
  (22 shorter events, 3.2 us)
Async XLA Ops:
  6.5 39.1 %all-gather.3.cloned.1.call-start = ((), (), s32[]{:S(2)}) async-start(), calls=%async_computation | async-start | bytes 2359296 | tf_op jit(solution)/shard_map/all_gather | solution.py:32
  9.4 104.1 %all-reduce.7.cloned.1.call-start = ((), (), s32[]{:S(2)}) async-start(), calls=%async_computation.1 | async-start | bytes 2097152 | tf_op jit(solution)/shard_map/psum | solution.py:48
  53.5 3.2 copy-start
  60.2 120.9 %all-reduce.9.cloned.1.call-start = ((), (), s32[]{:S(2)}) async-start(), calls=%async_computation.2 | async-start | bytes 2097152 | tf_op jit(solution)/shard_map/psum | solution.py:61
  122.4 127.6 %all-reduce.11.cloned.1.call-start = ((), (), s32[]{:S(2)}) async-start(), calls=%async_computation.3 | async-start | bytes 2097152 | tf_op jit(solution)/shard_map/psum | solution.py:48
  200.0 118.3 %all-reduce.13.cloned.1.call-start = ((), (), s32[]{:S(2)}) async-start(), calls=%async_computation.4 | async-start | bytes 2097152 | tf_op jit(solution)/shard_map/psum | solution.py:61
Sparse Core Ops, SparseCore 0:
  9.6 36.0 all-gather.2
  60.3 52.8 all-reduce.6
  122.5 58.5 all-reduce.8
  200.2 49.8 all-reduce.10
  259.0 59.2 all-reduce.12
where the time goes:
time: 338 us
  waiting for transfers between devices  169 us (50%)
  blocking collectives  102 us (30%)
  matrix products  36.3 us (11%)
  between operations  13.9 us (4%)
  other arithmetic  12.6 us (4%)
    psum x2, waiting for transfers between devices, local(): image = lax.psum(partial_rows, 'lm')  118 us
    psum x2, waiting for transfers between devices, local(): lax.psum(jnp.einsum('rl,rv->lv', build_tile, group_weighted, preferred_el...  50 us
    psum x1, blocking collectives, local(): totals = lax.psum(jnp.sum(weighted_full, axis=0), ('grp', 'lm'))  40.3 us
    psum x2, blocking collectives, local(): lax.psum((jnp.sum(image * image, axis=0), jnp.sum(weights[:, None] * imag...  19.7 us
    all_gather x1, blocking collectives, local(): lax.all_gather(weighted_full.astype(jnp.bfloat16), 'lm', axis=0, tiled=True)  17.3 us
    dot_general x2, matrix products, local(): jnp.dot(build_tile, side_b, preferred_element_type=jnp.float32)  14.1 us
    all_gather x1, blocking collectives, local(): lax.all_gather(row_weight.astype(jnp.bfloat16), 'lm', axis=0, tiled=True)  13.5 us
    psum x1, blocking collectives, local(): mean_sum, weight_sum = lax.psum((sums, jnp.sum(weights)), 'grp')  11.7 us
  transfers between devices with their start and end apart: 5, of which 4 were waited for; matrix products, arithmetic and copies ran while one was open for 1% of the time, Pallas kernels for 0%

commit v1 on v0

--- a/solution.py
+++ b/solution.py
@@ -41,7 +41,7 @@
     means = mean_sum / weight_sum
     vectors = start_vectors
     weighted_full = row_weight[:, None] * vectors
-    totals = lax.psum(jnp.sum(weighted_full, axis=0), ("grp", "lm"))
+    totals = jnp.sum(lax.all_gather(jnp.sum(weighted_full, axis=0), axis_name=("grp", "lm")), 0)
     group_weighted = lax.all_gather(weighted_full.astype(jnp.bfloat16), "lm", axis=0, tiled=True)
     for step in range(ITERS):
         side = (

time: 338 us -> 338 us (level)
    psum x1 -> x0, blocking collectives: 40.3 us -> none  [local(): totals = lax.psum(jnp.sum(weighted_full, axis=0), ('grp', 'lm'))]
    all_gather x0 -> x1, blocking collectives: none -> 40 us  [local(): lax.all_gather(jnp.sum(weighted_full, axis=0), axis_name=('grp', 'lm'))]
  transfers between devices with their start and end apart: 5 -> 5, of which waited for: 4 -> 5; matrix products, arithmetic and copies ran while one was open for 1% -> 2% of each run, Pallas kernels for 0% -> 0%
where the time goes in v1:
time: 338 us; the launch traced here: 337 us
  waiting for transfers between devices  172 us (51%)
  blocking collectives  99.1 us (29%)
  matrix products  36.2 us (11%)
  between operations  13.9 us (4%)
  other arithmetic  12.7 us (4%)
    psum x2, waiting for transfers between devices, local(): image = lax.psum(partial_rows, 'lm')  118 us
    psum x2, waiting for transfers between devices, local(): lax.psum(jnp.einsum('rl,rv->lv', build_tile, group_weighted, preferred_el...  52.3 us
    all_gather x1, blocking collectives, local(): lax.all_gather(jnp.sum(weighted_full, axis=0), axis_name=('grp', 'lm'))  40 us
    psum x2, blocking collectives, local(): lax.psum((jnp.sum(image * image, axis=0), jnp.sum(weights[:, None] * imag...  19.7 us
    all_gather x1, blocking collectives, local(): lax.all_gather(weighted_full.astype(jnp.bfloat16), 'lm', axis=0, tiled=True)  17.3 us
    dot_general x2, matrix products, local(): jnp.dot(build_tile, side_b, preferred_element_type=jnp.float32)  14.1 us
    all_gather x1, blocking collectives, local(): lax.all_gather(row_weight.astype(jnp.bfloat16), 'lm', axis=0, tiled=True)  13.5 us
    dot_general x2, matrix products, local(): jnp.einsum('rl,rv->lv', build_tile, group_weighted, preferred_element_typ...  10.7 us
  transfers between devices with their start and end apart: 5, of which 5 were waited for; matrix products, arithmetic and copies ran while one was open for 2% of the time, Pallas kernels for 0%

profile of v1, /device:TPU:0, one launch (start us, length us, event | category | flops | bytes accessed | tf_op | source)
XLA Modules:
  0.0 337.1 jit_solution(10633857802084797743)
XLA Ops:
  6.5 1.1 fusion.8
  7.6 1.8 fusion.9
  10.2 13.5 %all-gather.1 = bf16[8,1,256]{2,1,0:T(2,128)(2,1)S(1)} all-gather(bf16[1,1,256]{2,1,0:T(2,128)(2,1)S(1)} %reshape.22), channel_id=1, replica_groups=mesh['grp'=4,'lm'=8] {'lm'}, dimensions={0}, use_global_device_ids=true | all-gather | bytes 4608 | tf_op jit(solution)/shard_map/all_gather | solution.py:33
  24.3 2.1 fusion.1
  27.4 17.3 %all_gather.17 = bf16[2048,128]{1,0:T(8,128)(2,1)S(1)} all-gather(bf16[256,128]{1,0:T(8,128)(2,1)S(1)} %get-tuple-element.14), channel_id=1, replica_groups=mesh['grp'=4,'lm'=8] {'lm'}, dimensions={0}, use_global_device_ids=true | all-gather | bytes 589824 | tf_op jit(solution)/shard_map/all_gather | solution.py:45
  45.7 7.8 %multiply_reduce_fusion = (f32[2048]{0:T(1024)S(1)}, bf16[2048,2048]{1,0:T(8,128)(2,1)S(1)}) fusion(f32[2048]{0:T(1024)S(1)} %bitcast.20, f32[]{:T(128)} %bitcast.17, bf16[2048,512]{1,0:T(8,128)(2,1)} %all-gather.5.cloned.1.call-done, bf16[2048,512]{1,0:T(8,128)(2,1)} %param.6, f32[2048]{0:T(1024)S(1)} %add_rsqrt_fusion), kind=kOutput, calls=%fused_computation | convolution fusion | flops 4314888192 | bytes 12607492 | tf_op jit(solution)/shard_map/rd,ld->rl/dot_general | solution.py:16
  53.5 3.2 copy-done
  56.7 3.4 %fusion.14 = f32[2048,128]{1,0:T(8,128)} fusion(bf16[2048,2048]{1,0:T(8,128)(2,1)S(1)} %get-tuple-element.12, bf16[2048,128]{1,0:T(8,128)(2,1)S(1)} %all_gather.17), kind=kOutput, calls=%fused_computation.38 | convolution fusion | flops 1073741824 | bytes 9961472 | tf_op jit(solution)/shard_map/rl,rv->lv/dot_general | solution.py:49
  60.2 40.0 %all-gather.2 = f32[32,1,128]{2,1,0:T(1,128)S(1)} all-gather(f32[1,1,128]{2,1,0:T(1,128)S(1)} %bitcast.25), channel_id=2, replica_groups=mesh['grp'=4,'lm'=8] {'grp','lm'}, dimensions={0}, use_global_device_ids=true | all-gather | bytes 16896 | tf_op jit(solution)/shard_map/all_gather | solution.py:44
  100.8 8.6 %all-reduce.1 = (f32[2048]{0:T(1024)S(1)}, f32[]{:T(128)}) all-reduce(f32[2048]{0:T(1024)S(1)} %get-tuple-element.11, f32[]{:T(128)} %convert_reduce_fusion), channel_id=1, replica_groups=mesh['grp'=4,'lm'=8] {'grp'}, use_global_device_ids=true, to_apply=%region_4.0 | all-reduce | flops 2049 | bytes 16392 | tf_op jit(solution)/shard_map/psum | solution.py:40
  110.1 2.4 all-reduce.7.cloned.1.call-done
  112.5 1.8 convolution_bitcast_fusion.1
  114.3 7.1 %fusion.4 = f32[2048,128]{1,0:T(8,128)} fusion(bf16[2048,2048]{1,0:T(8,128)(2,1)} %copy-done, f32[128]{0:T(128)S(1)} %convolution_bitcast_fusion.1, f32[2048]{0:T(1024)S(1)} %bitcast.21, f32[2048,128]{1,0:T(8,128)} %all-reduce.7.cloned.1.call-done, f32[128]{0:T(128)S(1)} %reduce_sum.86, f32[2048]{0:T(1024)S(1)} %broadcast_divide_fusion), kind=kOutput, calls=%fused_computation.10 | convolution fusion | flops 1075052544 | bytes 10503168 | tf_op jit(solution)/shard_map/dot_general | solution.py:59
  121.5 59.0 %all-reduce.9.cloned.1.call-done = f32[2048,128]{1,0:T(8,128)} async-done(((f32[2048,128]{1,0:T(8,128)}), f32[2048,128]{1,0:T(8,128)}) %all-reduce.9.cloned.1.call-update) | async-done | bytes 1048592 | tf_op jit(solution)/shard_map/psum | solution.py:61
  180.4 1.6 multiply_reduce_fusion.2
  182.0 10.0 %all-reduce = (f32[128]{0:T(128)S(1)}, f32[128]{0:T(128)S(1)}) all-reduce(f32[128]{0:T(128)S(1)} %get-tuple-element.6, f32[128]{0:T(128)S(1)} %get-tuple-element.5), channel_id=1, replica_groups=mesh['grp'=4,'lm'=8] {'grp'}, use_global_device_ids=true, to_apply=%region_11.0 | all-reduce | flops 256 | bytes 2048 | tf_op jit(solution)/shard_map/psum | solution.py:62
  192.0 7.3 %fusion.10 = f32[2048,128]{1,0:T(8,128)} fusion(bf16[2048,2048]{1,0:T(8,128)(2,1)} %copy-done, f32[2048,128]{1,0:T(8,128)} %all-reduce.9.cloned.1.call-done, f32[128]{0:T(128)S(1)} %get-tuple-element.16, f32[2048]{0:T(1024)S(1)} %bitcast.23), kind=kOutput, calls=%fused_computation.25 | convolution fusion | flops 1074528256 | bytes 10494464 | tf_op jit(solution)/shard_map/rl,rv->lv/dot_general | solution.py:49
  199.4 49.9 %all-reduce.11.cloned.1.call-done = f32[2048,128]{1,0:T(8,128)} async-done(((f32[2048,128]{1,0:T(8,128)}), f32[2048,128]{1,0:T(8,128)}) %all-reduce.11.cloned.1.call-update) | async-done | bytes 1048592 | tf_op jit(solution)/shard_map/psum | solution.py:48
  249.3 1.8 convolution_bitcast_fusion
  251.1 7.1 %fusion.3 = f32[2048,128]{1,0:T(8,128)} fusion(bf16[2048,2048]{1,0:T(8,128)(2,1)} %copy-done, f32[128]{0:T(128)S(1)} %convolution_bitcast_fusion, f32[2048]{0:T(1024)S(1)} %bitcast.24, f32[2048,128]{1,0:T(8,128)} %all-reduce.11.cloned.1.call-done, f32[128]{0:T(128)S(1)} %get-tuple-element.15, f32[2048]{0:T(1024)S(1)} %broadcast_divide_fusion), kind=kOutput, calls=%fused_computation.8 | convolution fusion | flops 1075052544 | bytes 10503168 | tf_op jit(solution)/shard_map/dot_general | solution.py:59
  258.2 59.5 %all-reduce.13.cloned.1.call-done = f32[2048,128]{1,0:T(8,128)} async-done(((f32[2048,128]{1,0:T(8,128)}), f32[2048,128]{1,0:T(8,128)}) %all-reduce.13.cloned.1.call-update) | async-done | bytes 1048592 | tf_op jit(solution)/shard_map/psum | solution.py:61
  317.7 1.5 multiply_reduce_fusion.1
  319.2 9.8 %psum.71 = f32[128]{0:T(128)S(1)} all-reduce(f32[128]{0:T(128)S(1)} %multiply_reduce_fusion.1), channel_id=1, replica_groups=mesh['grp'=4,'lm'=8] {'grp'}, use_global_device_ids=true, to_apply=%region_17.0 | all-reduce | flops 128 | bytes 1024 | tf_op jit(solution)/shard_map/psum | solution.py:62
  329.0 1.6 dynamic-slice_divide_fusion
  (23 shorter events, 4.3 us)
Async XLA Ops:
  6.5 39.1 %all-gather.5.cloned.1.call-start = ((), (), s32[]{:S(2)}) async-start(), calls=%async_computation | async-start | bytes 2359296 | tf_op jit(solution)/shard_map/all_gather | solution.py:32
  9.4 103.1 %all-reduce.7.cloned.1.call-start = ((), (), s32[]{:S(2)}) async-start(), calls=%async_computation.1 | async-start | bytes 2097152 | tf_op jit(solution)/shard_map/psum | solution.py:48
  53.5 3.2 copy-start
  60.1 120.3 %all-reduce.9.cloned.1.call-start = ((), (), s32[]{:S(2)}) async-start(), calls=%async_computation.2 | async-start | bytes 2097152 | tf_op jit(solution)/shard_map/psum | solution.py:61
  121.4 127.9 %all-reduce.11.cloned.1.call-start = ((), (), s32[]{:S(2)}) async-start(), calls=%async_computation.3 | async-start | bytes 2097152 | tf_op jit(solution)/shard_map/psum | solution.py:48
  199.4 118.3 %all-reduce.13.cloned.1.call-start = ((), (), s32[]{:S(2)}) async-start(), calls=%async_computation.4 | async-start | bytes 2097152 | tf_op jit(solution)/shard_map/psum | solution.py:61
Sparse Core Ops, SparseCore 0:
  9.6 36.0 all-gather.4
  60.2 52.2 all-reduce.6
  121.6 58.8 all-reduce.8
  199.5 49.7 all-reduce.10
  258.3 59.2 all-reduce.12
